TPU v7x, 512 devices: a whole 4x8x8 slice. The times are simulated.
512 devices in a mesh: dp: 32 (over x, z_lo, core), seq: 16 (over z_hi, y).
Axes of the slice: x: 4, y: 8, z: 8 (z_hi: 2, z_lo: 4; z = z_hi * 4 + z_lo), core: 2. Of those that a mesh axis runs over, the one named last changes fastest.
Arguments:
- q_space: bfloat16 [32, 2560, 1152], P('dp', 'seq'), may hold values from -64 to 64
- k_space: bfloat16 [32, 2560, 1152], P('dp', 'seq'), may hold values from -6 to 6
- v_space: bfloat16 [32, 2560, 1152], P('dp', 'seq'), may hold values from -6 to 6
- q_time: bfloat16 [32, 2560, 1152], P('dp', 'seq'), may hold values from -64 to 64
- k_time: bfloat16 [32, 2560, 1152], P('dp', 'seq'), may hold values from -6 to 6
- v_time: bfloat16 [32, 2560, 1152], P('dp', 'seq'), may hold values from -6 to 6
- weight: bfloat16 [1152, 1152], P('dp'), may hold values from -0.1875 to 0.1875
- target: bfloat16 [32, 2560, 1152], P('dp', 'seq'), may hold values from -6 to 6
Outputs:
- grad_q_space: bfloat16 [32, 2560, 1152], P('dp', 'seq')
- grad_k_space: bfloat16 [32, 2560, 1152], P('dp', 'seq')
- grad_v_space: bfloat16 [32, 2560, 1152], P('dp', 'seq')
- grad_q_time: bfloat16 [32, 2560, 1152], P('dp', 'seq')
- grad_k_time: bfloat16 [32, 2560, 1152], P('dp', 'seq')
- grad_v_time: bfloat16 [32, 2560, 1152], P('dp', 'seq')
- weight_grad: float32 [1152, 1152], P('seq')
All inputs are finite; a program needn't handle non-finite values.
Results may differ from a plain program's by a relative error of at most 0.025.
Values may be sent and summed in bfloat16 or wider, within the bound.
A program may use at most 64 MiB of HBM per device.

v0:
```python
import math
import jax
import jax.numpy as jnp
from jax import lax
from jax.sharding import PartitionSpec as P

HEAD_DIM = 72


def form_pair(layout):
    if layout == "space":
        return ("blhe", "bmhe")
    return ("lbhe", "mbhe")


def split_heads(array):
    return array.reshape(array.shape[:-1] + (array.shape[-1] // HEAD_DIM, HEAD_DIM))


def attend_forward(query, key_data, values, layout):
    query_form, key_form = form_pair(layout)
    scaling = 1.0 / math.sqrt(HEAD_DIM)
    logits = (
        jnp.einsum(
            query_form + "," + key_form + "->bhlm",
            query,
            key_data,
            preferred_element_type=jnp.float32,
        )
        * scaling
    )
    row_max = jnp.max(logits, axis=-1, keepdims=True)
    lifted = jnp.exp(logits - row_max)
    attention = lifted / jnp.sum(lifted, axis=-1, keepdims=True)
    rounded = attention.astype(jnp.bfloat16)
    result = jnp.einsum(
        "bhlm," + key_form + "->" + query_form, rounded, values, preferred_element_type=jnp.float32
    )
    return (attention, rounded, result)


def attend_backward(query, key_data, values, attention, rounded, step_grad, layout):
    query_form, key_form = form_pair(layout)
    scaling = 1.0 / math.sqrt(HEAD_DIM)
    upstream = jnp.einsum(
        query_form + "," + key_form + "->bhlm",
        step_grad,
        values,
        preferred_element_type=jnp.float32,
    )
    grad_values = jnp.einsum(
        "bhlm," + query_form + "->" + key_form,
        rounded,
        step_grad,
        preferred_element_type=jnp.float32,
    ).astype(jnp.bfloat16)
    grad_scores = (
        attention * (upstream - jnp.sum(attention * upstream, axis=-1, keepdims=True))
    ).astype(jnp.bfloat16)
    grad_query = (
        jnp.einsum(
            "bhlm," + key_form + "->" + query_form,
            grad_scores,
            key_data,
            preferred_element_type=jnp.float32,
        )
        * scaling
    ).astype(jnp.bfloat16)
    grad_keys = (
        jnp.einsum(
            "bhlm," + query_form + "->" + key_form,
            grad_scores,
            query,
            preferred_element_type=jnp.float32,
        )
        * scaling
    ).astype(jnp.bfloat16)
    return (grad_query, grad_keys, grad_values)


def time_side(time_q, time_k, time_v, out_space, target_rows, full_weight):
    heads_q = split_heads(time_q)
    heads_k = split_heads(time_k)
    heads_v = split_heads(time_v)
    attention_t, rounded_t, result_t = attend_forward(heads_q, heads_k, heads_v, "time")
    combined = (out_space.astype(jnp.float32) + result_t.reshape(out_space.shape)).astype(
        jnp.bfloat16
    )
    projected = jnp.einsum("fnd,dc->fnc", combined, full_weight, preferred_element_type=jnp.float32)
    output_grad = (projected - target_rows.astype(jnp.float32)).astype(jnp.bfloat16)
    step_grad = jnp.einsum(
        "fnc,dc->fnd", output_grad, full_weight, preferred_element_type=jnp.float32
    ).astype(jnp.bfloat16)
    grads_time = attend_backward(
        heads_q, heads_k, heads_v, attention_t, rounded_t, split_heads(step_grad), "time"
    )
    grad_q, grad_k, grad_v = [item.reshape(out_space.shape) for item in grads_time]
    return (step_grad, grad_q, grad_k, grad_v, combined, output_grad)


def shards(q_space, k_space, v_space, q_time, k_time, v_time, weight, target):
    space_q = split_heads(q_space)
    space_k = split_heads(k_space)
    space_v = split_heads(v_space)
    attention_s, rounded_s, result_s = attend_forward(space_q, space_k, space_v, "space")
    out_space = result_s.astype(jnp.bfloat16).reshape(q_space.shape)
    full_weight = lax.all_gather(weight, "dp", axis=0, tiled=True)
    groups = lax.axis_size("seq")
    width = q_space.shape[2]
    per_block = q_space.shape[1] // groups

    def blocked(array):
        return array.reshape(1, groups, per_block, width)

    def per_patch(pieces):
        flat = [item[:, 0] for item in pieces]
        outcome = time_side(flat[0], flat[1], flat[2], flat[3], flat[4], full_weight)
        return tuple((item[:, None] for item in outcome))

    mapped = per_patch(
        (
            lax.all_to_all(blocked(q_time), "seq", split_axis=1, concat_axis=0, tiled=True),
            lax.all_to_all(blocked(k_time), "seq", split_axis=1, concat_axis=0, tiled=True),
            lax.all_to_all(blocked(v_time), "seq", split_axis=1, concat_axis=0, tiled=True),
            lax.all_to_all(blocked(out_space), "seq", split_axis=1, concat_axis=0, tiled=True),
            lax.all_to_all(blocked(target), "seq", split_axis=1, concat_axis=0, tiled=True),
        )
    )
    returned = tuple((item[:, 0] for item in mapped))
    step_grad, grad_qt, grad_kt, grad_vt, combined, output_grad = returned
    home = (
        lax.all_to_all(step_grad, "seq", split_axis=0, concat_axis=1, tiled=True),
        lax.all_to_all(grad_qt, "seq", split_axis=0, concat_axis=1, tiled=True),
        lax.all_to_all(grad_kt, "seq", split_axis=0, concat_axis=1, tiled=True),
        lax.all_to_all(grad_vt, "seq", split_axis=0, concat_axis=1, tiled=True),
    )
    grads_space = attend_backward(
        space_q, space_k, space_v, attention_s, rounded_s, split_heads(home[0]), "space"
    )
    grad_qs, grad_ks, grad_vs = [item.reshape(q_space.shape) for item in grads_space]
    flat_comb = combined.reshape(-1, combined.shape[-1])
    flat_grad = output_grad.reshape(-1, output_grad.shape[-1])
    share = lax.psum_scatter(
        lax.dot_general(
            flat_comb, flat_grad, (((0,), (0,)), ((), ())), preferred_element_type=jnp.float32
        ).astype(jnp.bfloat16),
        "seq",
        scatter_dimension=0,
        tiled=True,
    )
    total = lax.psum(share, "dp").astype(jnp.float32)
    scaling = 1.0 / math.sqrt(lax.axis_size("dp") * lax.axis_size("seq") * q_space.shape[1])
    return (grad_qs, grad_ks, grad_vs, home[1], home[2], home[3], total * scaling)


def solution(mesh):
    return jax.shard_map(
        shards,
        mesh=mesh,
        in_specs=(
            P("dp", "seq", None),
            P("dp", "seq", None),
            P("dp", "seq", None),
            P("dp", "seq", None),
            P("dp", "seq", None),
            P("dp", "seq", None),
            P("dp", None),
            P("dp", "seq", None),
        ),
        out_specs=(
            P("dp", "seq", None),
            P("dp", "seq", None),
            P("dp", "seq", None),
            P("dp", "seq", None),
            P("dp", "seq", None),
            P("dp", "seq", None),
            P("seq", None),
        ),
        check_vma=False,
    )
```

profile of v0, /device:TPU:8, one launch (start us, length us, event | category | flops | bytes accessed | tf_op | source)
XLA Modules:
  0.0 651.9 jit_solution(3526886626338543197)
XLA Ops:
  7.9 1.9 reshape.158
  9.9 16.0 %all-to-all-start.1 = ((bf16[1,16,10,1152]{3,2,0,1:T(8,128)(2,1)}), bf16[1,16,10,1152]{3,2,0,1:T(8,128)(2,1)S(1)}, u32[]{:S(2)}, u32[]{:S(2)}) async-start(bf16[1,16,10,1152]{3,2,0,1:T(8,128)(2,1)} %bitcast.5), calls=%async_computation.1 | async-start | bytes 1179648 | tf_op jit(solution)/shard_map/all_to_all | solution.py:122
  26.8 19.1 %all-to-all-done.1 = bf16[1,16,10,1152]{3,2,0,1:T(8,128)(2,1)S(1)} async-done(((bf16[1,16,10,1152]{3,2,0,1:T(8,128)(2,1)}), bf16[1,16,10,1152]{3,2,0,1:T(8,128)(2,1)S(1)}, u32[]{:S(2)}, u32[]{:S(2)}) %all-to-all-start.1) | async-done | bytes 368672 | tf_op jit(solution)/shard_map/all_to_all | solution.py:122
  45.9 6.0 all-to-all-start.2
  55.3 16.6 %all-to-all-done.2 = bf16[1,16,10,1152]{3,2,0,1:T(8,128)(2,1)S(1)} async-done(((bf16[1,16,10,1152]{3,2,0,1:T(8,128)(2,1)}), bf16[1,16,10,1152]{3,2,0,1:T(8,128)(2,1)S(1)}, u32[]{:S(2)}, u32[]{:S(2)}) %all-to-all-start.2) | async-done | bytes 368672 | tf_op jit(solution)/shard_map/all_to_all | solution.py:123
  72.0 6.0 all-to-all-start.3
  77.9 2.2 fusion.50
  80.1 2.7 fusion.17
  86.2 10.9 %all-to-all-done.3 = bf16[1,16,10,1152]{3,2,0,1:T(8,128)(2,1)} async-done(((bf16[1,16,10,1152]{3,2,0,1:T(8,128)(2,1)}), bf16[1,16,10,1152]{3,2,0,1:T(8,128)(2,1)}, u32[]{:S(2)}, u32[]{:S(2)}) %all-to-all-start.3) | async-done | bytes 368672 | tf_op jit(solution)/shard_map/all_to_all | solution.py:124
  97.1 6.6 %all-to-all-start = ((bf16[1,16,10,1152]{3,2,0,1:T(8,128)(2,1)}), bf16[1,16,10,1152]{3,2,0,1:T(8,128)(2,1)S(1)}, u32[]{:S(2)}, u32[]{:S(2)}) async-start(bf16[1,16,10,1152]{3,2,0,1:T(8,128)(2,1)} %bitcast.3), calls=%async_computation | async-start | bytes 1179648 | tf_op jit(solution)/shard_map/all_to_all | solution.py:125
  107.1 2.6 reshape.181
  109.7 2.0 fusion.45
  111.7 10.1 %all-to-all-done = bf16[1,16,10,1152]{3,2,0,1:T(8,128)(2,1)S(1)} async-done(((bf16[1,16,10,1152]{3,2,0,1:T(8,128)(2,1)}), bf16[1,16,10,1152]{3,2,0,1:T(8,128)(2,1)S(1)}, u32[]{:S(2)}, u32[]{:S(2)}) %all-to-all-start) | async-done | bytes 368672 | tf_op jit(solution)/shard_map/all_to_all | solution.py:125
  121.8 5.7 all-to-all-start.4
  131.4 3.6 reshape.172
  135.0 9.6 %all-to-all-done.4 = bf16[1,16,10,1152]{3,2,0,1:T(8,128)(2,1)S(1)} async-done(((bf16[1,16,10,1152]{3,2,0,1:T(8,128)(2,1)}), bf16[1,16,10,1152]{3,2,0,1:T(8,128)(2,1)S(1)}, u32[]{:S(2)}, u32[]{:S(2)}) %all-to-all-start.4) | async-done | bytes 368672 | tf_op jit(solution)/shard_map/all_to_all | solution.py:126
  147.1 2.5 fusion.2
  152.5 5.5 all-to-all-start.5
  162.2 2.8 multiply_reduce_fusion.2
  165.0 11.3 %all-to-all-done.5 = bf16[16,10,1152]{2,1,0:T(8,128)(2,1)S(1)} async-done(((bf16[16,10,1152]{2,1,0:T(8,128)(2,1)}), bf16[16,10,1152]{2,1,0:T(8,128)(2,1)S(1)}, u32[]{:S(2)}, u32[]{:S(2)}) %all-to-all-start.5) | async-done | bytes 368672 | tf_op jit(solution)/shard_map/all_to_all | solution.py:132
  176.3 5.6 all-to-all-start.8
  188.5 2.5 reshape.163
  192.5 10.1 %all-to-all-done.8 = bf16[16,10,1152]{2,1,0:T(8,128)(2,1)} async-done(((bf16[16,10,1152]{2,1,0:T(8,128)(2,1)}), bf16[16,10,1152]{2,1,0:T(8,128)(2,1)}, u32[]{:S(2)}, u32[]{:S(2)}) %all-to-all-start.8) | async-done | bytes 368672 | tf_op jit(solution)/shard_map/all_to_all | solution.py:135
  202.6 5.6 all-to-all-start.7
  208.3 2.0 multiply_reduce_fusion
  210.9 19.1 %all-to-all-done.7 = bf16[16,10,1152]{2,1,0:T(8,128)(2,1)S(1)} async-done(((bf16[16,10,1152]{2,1,0:T(8,128)(2,1)}), bf16[16,10,1152]{2,1,0:T(8,128)(2,1)S(1)}, u32[]{:S(2)}, u32[]{:S(2)}) %all-to-all-start.7) | async-done | bytes 368672 | tf_op jit(solution)/shard_map/all_to_all | solution.py:134
  229.9 4.8 all-to-all-start.6
  234.8 3.2 convolution_convert_fusion.2
  238.0 2.0 copy.119
  241.4 139.1 %reduce-scatter.4.cloned.1.call-done = bf16[72,1152]{1,0:T(8,128)(2,1)} async-done(((bf16[1152,1152]{1,0:T(8,128)(2,1)}), bf16[72,1152]{1,0:T(8,128)(2,1)}) %reduce-scatter.4.cloned.1.call-update) | async-done | bytes 165904
  384.8 1.9 all_to_all.31
  386.7 257.0 %all-reduce.3.cloned.1.call-done = bf16[72,1152]{1,0:T(8,128)(2,1)} async-done(((bf16[72,1152]{1,0:T(8,128)(2,1)}), bf16[72,1152]{1,0:T(8,128)(2,1)}) %all-reduce.3.cloned.1.call-update) | async-done | bytes 165904 | tf_op jit(solution)/shard_map/psum | solution.py:151
  (107 shorter events, 41.1 us)
Async XLA Ops:
  7.2 18.7 %copy-start.25 = (bf16[1,160,1152]{2,1,0:T(8,128)(2,1)S(1)}, bf16[1,160,1152]{2,1,0:T(8,128)(2,1)}, u32[]{:S(2)}) copy-start(bf16[1,160,1152]{2,1,0:T(8,128)(2,1)} %param.12) | copy-start | bytes 1105924
  7.2 124.2 %all-gather.3.cloned.1.call-start = ((), (), s32[]{:S(2)}) async-start(), calls=%async_computation.11 | async-start | bytes 3041280 | tf_op jit(solution)/shard_map/all_gather | solution.py:107
  9.9 36.1 %all-to-all-start.1 = ((bf16[1,16,10,1152]{3,2,0,1:T(8,128)(2,1)}), bf16[1,16,10,1152]{3,2,0,1:T(8,128)(2,1)S(1)}, u32[]{:S(2)}, u32[]{:S(2)}) async-start(bf16[1,16,10,1152]{3,2,0,1:T(8,128)(2,1)} %bitcast.5), calls=%async_computation.1 | async-start | bytes 1179648 | tf_op jit(solution)/shard_map/all_to_all | solution.py:122
  25.9 26.0 %copy-start.26 = (bf16[1,160,1152]{2,1,0:T(8,128)(2,1)S(1)}, bf16[1,160,1152]{2,1,0:T(8,128)(2,1)}, u32[]{:S(2)}) copy-start(bf16[1,160,1152]{2,1,0:T(8,128)(2,1)} %param.8) | copy-start | bytes 1105924
  25.9 26.3 %copy-start.27 = (bf16[1,160,1152]{2,1,0:T(8,128)(2,1)S(1)}, bf16[1,160,1152]{2,1,0:T(8,128)(2,1)}, u32[]{:S(2)}) copy-start(bf16[1,160,1152]{2,1,0:T(8,128)(2,1)} %param.9) | copy-start | bytes 1105924
  45.9 7.3 %copy-start.12 = (bf16[1,16,10,1152]{3,2,0,1:T(8,128)(2,1)}, bf16[1,16,10,1152]{3,2,0,1:T(8,128)(2,1)S(1)}, u32[]{:S(2)}) copy-start(bf16[1,16,10,1152]{3,2,0,1:T(8,128)(2,1)S(1)} %all-to-all-done.1) | copy-start | bytes 1105924
  45.9 7.3 %copy-start.28 = (bf16[1,160,1152]{2,1,0:T(8,128)(2,1)S(1)}, bf16[1,160,1152]{2,1,0:T(8,128)(2,1)}, u32[]{:S(2)}) copy-start(bf16[1,160,1152]{2,1,0:T(8,128)(2,1)} %param.10) | copy-start | bytes 1105924
  45.9 26.0 %all-to-all-start.2 = ((bf16[1,16,10,1152]{3,2,0,1:T(8,128)(2,1)}), bf16[1,16,10,1152]{3,2,0,1:T(8,128)(2,1)S(1)}, u32[]{:S(2)}, u32[]{:S(2)}) async-start(bf16[1,16,10,1152]{3,2,0,1:T(8,128)(2,1)} %bitcast.6), calls=%async_computation.2 | async-start | bytes 1179648 | tf_op jit(solution)/shard_map/all_to_all | solution.py:123
  52.1 25.8 %copy-start.7 = (bf16[1,160,1152]{1,2,0:T(8,128)(2,1)}, bf16[1,160,1152]{1,2,0:T(8,128)(2,1)S(1)}, u32[]{:S(2)}) copy-start(bf16[1,160,1152]{1,2,0:T(8,128)(2,1)S(1)} %copy.131) | copy-start | bytes 1105924
  71.9 6.0 copy-start.15
  72.0 25.1 %all-to-all-start.3 = ((bf16[1,16,10,1152]{3,2,0,1:T(8,128)(2,1)}), bf16[1,16,10,1152]{3,2,0,1:T(8,128)(2,1)}, u32[]{:S(2)}, u32[]{:S(2)}) async-start(bf16[1,16,10,1152]{3,2,0,1:T(8,128)(2,1)} %bitcast.7), calls=%async_computation.3 | async-start | bytes 1179648 | tf_op jit(solution)/shard_map/all_to_all | solution.py:124
  84.4 19.3 %copy-start.30 = (bf16[1,160,1152]{2,1,0:T(8,128)(2,1)S(1)}, bf16[1,160,1152]{2,1,0:T(8,128)(2,1)}, u32[]{:S(2)}) copy-start(bf16[1,160,1152]{2,1,0:T(8,128)(2,1)} %param.15) | copy-start | bytes 1105924
  86.2 18.5 %copy-start.13 = (bf16[1,16,10,1152]{3,2,0,1:T(8,128)(2,1)S(1)}, bf16[1,16,10,1152]{3,2,0,1:T(8,128)(2,1)}, u32[]{:S(2)}) copy-start(bf16[1,16,10,1152]{3,2,0,1:T(8,128)(2,1)} %copy-done.12) | copy-start | bytes 1105924
  97.1 24.7 %all-to-all-start = ((bf16[1,16,10,1152]{3,2,0,1:T(8,128)(2,1)}), bf16[1,16,10,1152]{3,2,0,1:T(8,128)(2,1)S(1)}, u32[]{:S(2)}, u32[]{:S(2)}) async-start(bf16[1,16,10,1152]{3,2,0,1:T(8,128)(2,1)} %bitcast.3), calls=%async_computation | async-start | bytes 1179648 | tf_op jit(solution)/shard_map/all_to_all | solution.py:125
  105.9 5.9 copy-start.3
  107.1 4.6 copy-start.5
  109.7 18.0 %copy-start.18 = (bf16[16,10,16,72]{3,2,1,0:T(8,128)(2,1)}, bf16[16,10,16,72]{3,2,1,0:T(8,128)(2,1)S(1)}, u32[]{:S(2)}) copy-start(bf16[16,10,16,72]{3,2,1,0:T(8,128)(2,1)S(1)} %reshape.181) | copy-start | bytes 1105924
  121.8 22.8 %all-to-all-start.4 = ((bf16[1,16,10,1152]{3,2,0,1:T(8,128)(2,1)}), bf16[1,16,10,1152]{3,2,0,1:T(8,128)(2,1)S(1)}, u32[]{:S(2)}, u32[]{:S(2)}) async-start(bf16[1,16,10,1152]{3,2,0,1:T(8,128)(2,1)} %bitcast.10), calls=%async_computation.4 | async-start | bytes 1179648 | tf_op jit(solution)/shard_map/all_to_all | solution.py:126
  127.5 252.9 %reduce-scatter.4.cloned.1.call-start = ((), (), s32[]{:S(2)}) async-start(), calls=%async_computation.12 | async-start | bytes 2820096
  152.5 7.5 %copy-start.17 = (f32[10,16,16,16]{2,3,1,0:T(8,128)S(1)}, f32[10,16,16,16]{2,3,1,0:T(8,128)}, u32[]{:S(2)}) copy-start(f32[10,16,16,16]{2,3,1,0:T(8,128)} %get-tuple-element.29) | copy-start | bytes 491524
  152.5 23.8 %all-to-all-start.5 = ((bf16[16,10,1152]{2,1,0:T(8,128)(2,1)}), bf16[16,10,1152]{2,1,0:T(8,128)(2,1)S(1)}, u32[]{:S(2)}, u32[]{:S(2)}) async-start(bf16[16,10,1152]{2,1,0:T(8,128)(2,1)} %copy.94), calls=%async_computation.5 | async-start | bytes 1179648 | tf_op jit(solution)/shard_map/all_to_all | solution.py:132
  176.3 7.3 %copy-start.14 = (bf16[16,10,1152]{2,1,0:T(8,128)(2,1)}, bf16[16,10,1152]{2,1,0:T(8,128)(2,1)S(1)}, u32[]{:S(2)}) copy-start(bf16[16,10,1152]{2,1,0:T(8,128)(2,1)S(1)} %all-to-all-done.5) | copy-start | bytes 1105924
  176.3 26.3 %all-to-all-start.8 = ((bf16[16,10,1152]{2,1,0:T(8,128)(2,1)}), bf16[16,10,1152]{2,1,0:T(8,128)(2,1)}, u32[]{:S(2)}, u32[]{:S(2)}) async-start(bf16[16,10,1152]{2,1,0:T(8,128)(2,1)} %reshape.177), calls=%async_computation.8 | async-start | bytes 1179648 | tf_op jit(solution)/shard_map/all_to_all | solution.py:135
  188.5 19.7 %copy-start.1 = (f32[16,160,160]{1,2,0:T(8,128)S(1)}, f32[16,160,160]{1,2,0:T(8,128)}, u32[]{:S(2)}) copy-start(f32[16,160,160]{1,2,0:T(8,128)} %copy-done) | copy-start | bytes 4915204
  202.6 27.3 %all-to-all-start.7 = ((bf16[16,10,1152]{2,1,0:T(8,128)(2,1)}), bf16[16,10,1152]{2,1,0:T(8,128)(2,1)S(1)}, u32[]{:S(2)}, u32[]{:S(2)}) async-start(bf16[16,10,1152]{2,1,0:T(8,128)(2,1)} %reshape.176), calls=%async_computation.7 | async-start | bytes 1179648 | tf_op jit(solution)/shard_map/all_to_all | solution.py:134
  210.4 24.5 %copy-start.21 = (bf16[160,16,72]{0,2,1:T(8,128)(2,1)S(1)}, bf16[160,16,72]{0,2,1:T(8,128)(2,1)}, u32[]{:S(2)}) copy-start(bf16[160,16,72]{0,2,1:T(8,128)(2,1)} %copy.95) | copy-start | bytes 1105924
  229.9 8.1 %copy-start.10 = (bf16[16,10,1152]{2,1,0:T(8,128)(2,1)}, bf16[16,10,1152]{2,1,0:T(8,128)(2,1)S(1)}, u32[]{:S(2)}) copy-start(bf16[16,10,1152]{2,1,0:T(8,128)(2,1)S(1)} %all-to-all-done.7) | copy-start | bytes 1105924
  229.9 154.8 %all-to-all-start.6 = ((bf16[16,10,1152]{2,1,0:T(8,128)(2,1)}), bf16[16,10,1152]{2,1,0:T(8,128)(2,1)}, u32[]{:S(2)}, u32[]{:S(2)}) async-start(bf16[16,10,1152]{2,1,0:T(8,128)(2,1)} %reshape.175), calls=%async_computation.6 | async-start | bytes 1179648 | tf_op jit(solution)/shard_map/all_to_all | solution.py:133
  234.7 5.3 copy-start.9
  234.8 409.0 %all-reduce.3.cloned.1.call-start = ((), (), s32[]{:S(2)}) async-start(), calls=%async_computation.10 | async-start | bytes 331776 | tf_op jit(solution)/shard_map/psum | solution.py:151
  240.1 140.4 %copy-start.8 = (bf16[1,160,1152]{1,2,0:T(8,128)(2,1)S(1)}, bf16[1,160,1152]{1,2,0:T(8,128)(2,1)}, u32[]{:S(2)}) copy-start(bf16[1,160,1152]{1,2,0:T(8,128)(2,1)} %copy-done.7) | copy-start | bytes 1105924
  381.0 2.9 copy-start.11
  (11 other events, 19.8 us)
Sparse Core Ops, SparseCore 0:
  10.2 94.6 all-gather.2
  149.8 230.5 reduce-scatter.3
  383.6 260.0 all-reduce.2
where the time goes:
time: 654 us; the launch traced here: 652 us
  waiting for transfers between devices  504 us (77%)
  starting transfers between devices  62.1 us (9%)
  local copies, waits for them, and re-layouts  43.3 us (7%)
  matrix products  24.1 us (4%)
  between operations  14.2 us (2%)
    psum x1, waiting for transfers between devices, shards(): total = lax.psum(share, 'dp').astype(jnp.float32)  257 us
    unnamed x4, waiting for transfers between devices  140 us
    all_to_all x1, waiting for transfers between devices, shards(): lax.all_to_all(blocked(q_time), 'seq', split_axis=1, concat_axis=0, tiled...  19.1 us
    all_to_all x1, waiting for transfers between devices, shards(): lax.all_to_all(grad_kt, 'seq', split_axis=0, concat_axis=1, tiled=True)  19.1 us
    all_to_all x1, waiting for transfers between devices, shards(): lax.all_to_all(blocked(k_time), 'seq', split_axis=1, concat_axis=0, tiled...  16.6 us
    all_to_all x1, starting transfers between devices, shards(): lax.all_to_all(blocked(q_time), 'seq', split_axis=1, concat_axis=0, tiled...  16 us
  transfers between devices with their start and end apart: 12, of which 10 were waited for; matrix products, arithmetic and copies ran while one was open for 9% of the time, Pallas kernels for 0%

commit v1 on v0

--- a/solution.py
+++ b/solution.py
@@ -148,7 +148,7 @@
         scatter_dimension=0,
         tiled=True,
     )
-    total = lax.psum(share, "dp").astype(jnp.float32)
+    total = jnp.sum(lax.all_gather(share, "dp"), axis=0).astype(jnp.float32)
     scaling = 1.0 / math.sqrt(lax.axis_size("dp") * lax.axis_size("seq") * q_space.shape[1])
     return (grad_qs, grad_ks, grad_vs, home[1], home[2], home[3], total * scaling)
 

time: 654 us -> 480 us (0.73)
  the two profiles are of different devices: /device:TPU:8 before, /device:TPU:17 now
where the time goes in v1:
time: 480 us; the launch traced here: 479 us
  waiting for transfers between devices  314 us (65%)
  starting transfers between devices  77 us (16%)
  local copies, waits for them, and re-layouts  42.3 us (9%)
  matrix products  24.2 us (5%)
  between operations  14.2 us (3%)
  other arithmetic  7.12 us (1%)
    unnamed x4, waiting for transfers between devices  219 us
    all_gather x1, waiting for transfers between devices, shards(): total = jnp.sum(lax.all_gather(share, 'dp'), axis=0).astype(jnp.float32)  22.3 us
    all_to_all x1, waiting for transfers between devices, shards(): lax.all_to_all(blocked(q_time), 'seq', split_axis=1, concat_axis=0, tiled...  16.9 us
    all_to_all x1, starting transfers between devices, shards(): lax.all_to_all(blocked(q_time), 'seq', split_axis=1, concat_axis=0, tiled...  15.3 us
    all_to_all x1, waiting for transfers between devices, shards(): lax.all_to_all(blocked(k_time), 'seq', split_axis=1, concat_axis=0, tiled...  12.5 us
    all_to_all x1, waiting for transfers between devices, shards(): lax.all_to_all(grad_kt, 'seq', split_axis=0, concat_axis=1, tiled=True)  11 us
  transfers between devices with their start and end apart: 12, of which 11 were waited for; matrix products, arithmetic and copies ran while one was open for 12% of the time, Pallas kernels for 0%

profile of v1, /device:TPU:17, one launch (start us, length us, event | category | flops | bytes accessed | tf_op | source)
XLA Modules:
  0.0 478.6 jit_solution(16375396406292847817)
XLA Ops:
  9.9 15.3 %all-to-all-start.1 = ((bf16[1,16,10,1152]{3,2,0,1:T(8,128)(2,1)}), bf16[1,16,10,1152]{3,2,0,1:T(8,128)(2,1)S(1)}, u32[]{:S(2)}, u32[]{:S(2)}) async-start(bf16[1,16,10,1152]{3,2,0,1:T(8,128)(2,1)} %bitcast.5), calls=%async_computation.1 | async-start | bytes 1179648 | tf_op jit(solution)/shard_map/all_to_all | solution.py:122
  26.2 16.9 %all-to-all-done.1 = bf16[1,16,10,1152]{3,2,0,1:T(8,128)(2,1)S(1)} async-done(((bf16[1,16,10,1152]{3,2,0,1:T(8,128)(2,1)}), bf16[1,16,10,1152]{3,2,0,1:T(8,128)(2,1)S(1)}, u32[]{:S(2)}, u32[]{:S(2)}) %all-to-all-start.1) | async-done | bytes 368672 | tf_op jit(solution)/shard_map/all_to_all | solution.py:122
  43.1 7.9 %all-to-all-start.2 = ((bf16[1,16,10,1152]{3,2,0,1:T(8,128)(2,1)}), bf16[1,16,10,1152]{3,2,0,1:T(8,128)(2,1)S(1)}, u32[]{:S(2)}, u32[]{:S(2)}) async-start(bf16[1,16,10,1152]{3,2,0,1:T(8,128)(2,1)} %bitcast.6), calls=%async_computation.2 | async-start | bytes 1179648 | tf_op jit(solution)/shard_map/all_to_all | solution.py:123
  54.4 12.5 %all-to-all-done.2 = bf16[1,16,10,1152]{3,2,0,1:T(8,128)(2,1)S(1)} async-done(((bf16[1,16,10,1152]{3,2,0,1:T(8,128)(2,1)}), bf16[1,16,10,1152]{3,2,0,1:T(8,128)(2,1)S(1)}, u32[]{:S(2)}, u32[]{:S(2)}) %all-to-all-start.2) | async-done | bytes 368672 | tf_op jit(solution)/shard_map/all_to_all | solution.py:123
  66.9 9.0 %all-to-all-start.3 = ((bf16[1,16,10,1152]{3,2,0,1:T(8,128)(2,1)}), bf16[1,16,10,1152]{3,2,0,1:T(8,128)(2,1)}, u32[]{:S(2)}, u32[]{:S(2)}) async-start(bf16[1,16,10,1152]{3,2,0,1:T(8,128)(2,1)} %bitcast.7), calls=%async_computation.3 | async-start | bytes 1179648 | tf_op jit(solution)/shard_map/all_to_all | solution.py:124
  75.9 2.2 fusion.50
  78.1 2.7 fusion.17
  84.2 6.5 %all-to-all-done.3 = bf16[1,16,10,1152]{3,2,0,1:T(8,128)(2,1)} async-done(((bf16[1,16,10,1152]{3,2,0,1:T(8,128)(2,1)}), bf16[1,16,10,1152]{3,2,0,1:T(8,128)(2,1)}, u32[]{:S(2)}, u32[]{:S(2)}) %all-to-all-start.3) | async-done | bytes 368672 | tf_op jit(solution)/shard_map/all_to_all | solution.py:124
  90.6 9.6 %all-to-all-start = ((bf16[1,16,10,1152]{3,2,0,1:T(8,128)(2,1)}), bf16[1,16,10,1152]{3,2,0,1:T(8,128)(2,1)S(1)}, u32[]{:S(2)}, u32[]{:S(2)}) async-start(bf16[1,16,10,1152]{3,2,0,1:T(8,128)(2,1)} %bitcast.3), calls=%async_computation | async-start | bytes 1179648 | tf_op jit(solution)/shard_map/all_to_all | solution.py:125
  103.6 2.6 reshape.182
  106.2 2.1 fusion.45
  108.3 6.1 %all-to-all-done = bf16[1,16,10,1152]{3,2,0,1:T(8,128)(2,1)S(1)} async-done(((bf16[1,16,10,1152]{3,2,0,1:T(8,128)(2,1)}), bf16[1,16,10,1152]{3,2,0,1:T(8,128)(2,1)S(1)}, u32[]{:S(2)}, u32[]{:S(2)}) %all-to-all-start) | async-done | bytes 368672 | tf_op jit(solution)/shard_map/all_to_all | solution.py:125
  114.4 9.2 %all-to-all-start.4 = ((bf16[1,16,10,1152]{3,2,0,1:T(8,128)(2,1)}), bf16[1,16,10,1152]{3,2,0,1:T(8,128)(2,1)S(1)}, u32[]{:S(2)}, u32[]{:S(2)}) async-start(bf16[1,16,10,1152]{3,2,0,1:T(8,128)(2,1)} %bitcast.10), calls=%async_computation.4 | async-start | bytes 1179648 | tf_op jit(solution)/shard_map/all_to_all | solution.py:126
  127.5 3.6 reshape.173
  131.0 6.0 %all-to-all-done.4 = bf16[1,16,10,1152]{3,2,0,1:T(8,128)(2,1)S(1)} async-done(((bf16[1,16,10,1152]{3,2,0,1:T(8,128)(2,1)}), bf16[1,16,10,1152]{3,2,0,1:T(8,128)(2,1)S(1)}, u32[]{:S(2)}, u32[]{:S(2)}) %all-to-all-start.4) | async-done | bytes 368672 | tf_op jit(solution)/shard_map/all_to_all | solution.py:126
  139.6 2.5 fusion.2
  142.2 218.4 %reduce-scatter.4.cloned.1.call-done = bf16[72,1152]{1,0:T(8,128)(2,1)} async-done(((bf16[1152,1152]{1,0:T(8,128)(2,1)}), bf16[72,1152]{1,0:T(8,128)(2,1)}) %reduce-scatter.4.cloned.1.call-update) | async-done | bytes 165904
  362.5 5.9 %all-to-all-start.5 = ((bf16[16,10,1152]{2,1,0:T(8,128)(2,1)}), bf16[16,10,1152]{2,1,0:T(8,128)(2,1)S(1)}, u32[]{:S(2)}, u32[]{:S(2)}) async-start(bf16[16,10,1152]{2,1,0:T(8,128)(2,1)} %copy.94), calls=%async_computation.5 | async-start | bytes 1179648 | tf_op jit(solution)/shard_map/all_to_all | solution.py:132
  372.6 2.9 multiply_reduce_fusion.2
  375.5 7.1 %all-to-all-done.5 = bf16[16,10,1152]{2,1,0:T(8,128)(2,1)S(1)} async-done(((bf16[16,10,1152]{2,1,0:T(8,128)(2,1)}), bf16[16,10,1152]{2,1,0:T(8,128)(2,1)S(1)}, u32[]{:S(2)}, u32[]{:S(2)}) %all-to-all-start.5) | async-done | bytes 368672 | tf_op jit(solution)/shard_map/all_to_all | solution.py:132
  382.6 5.6 %all-to-all-start.8 = ((bf16[16,10,1152]{2,1,0:T(8,128)(2,1)}), bf16[16,10,1152]{2,1,0:T(8,128)(2,1)}, u32[]{:S(2)}, u32[]{:S(2)}) async-start(bf16[16,10,1152]{2,1,0:T(8,128)(2,1)} %reshape.178), calls=%async_computation.8 | async-start | bytes 1179648 | tf_op jit(solution)/shard_map/all_to_all | solution.py:135
  394.8 2.5 reshape.163
  398.7 3.3 all-to-all-done.8
  402.0 8.3 %all-to-all-start.7 = ((bf16[16,10,1152]{2,1,0:T(8,128)(2,1)}), bf16[16,10,1152]{2,1,0:T(8,128)(2,1)S(1)}, u32[]{:S(2)}, u32[]{:S(2)}) async-start(bf16[16,10,1152]{2,1,0:T(8,128)(2,1)} %reshape.177), calls=%async_computation.7 | async-start | bytes 1179648 | tf_op jit(solution)/shard_map/all_to_all | solution.py:134
  410.3 2.0 multiply_reduce_fusion
  412.9 11.0 %all-to-all-done.7 = bf16[16,10,1152]{2,1,0:T(8,128)(2,1)S(1)} async-done(((bf16[16,10,1152]{2,1,0:T(8,128)(2,1)}), bf16[16,10,1152]{2,1,0:T(8,128)(2,1)S(1)}, u32[]{:S(2)}, u32[]{:S(2)}) %all-to-all-start.7) | async-done | bytes 368672 | tf_op jit(solution)/shard_map/all_to_all | solution.py:134
  423.9 6.0 %all-to-all-start.6 = ((bf16[16,10,1152]{2,1,0:T(8,128)(2,1)}), bf16[16,10,1152]{2,1,0:T(8,128)(2,1)}, u32[]{:S(2)}, u32[]{:S(2)}) async-start(bf16[16,10,1152]{2,1,0:T(8,128)(2,1)} %reshape.176), calls=%async_computation.6 | async-start | bytes 1179648 | tf_op jit(solution)/shard_map/all_to_all | solution.py:133
  429.9 3.2 convolution_convert_fusion.2
  433.1 2.0 copy.119
  440.8 3.0 all-to-all-done.6
  445.7 22.3 %all-gather.5.cloned.1.call-done = bf16[2304,1152]{1,0:T(8,128)(2,1)} async-done(((bf16[72,1152]{1,0:T(8,128)(2,1)}), bf16[2304,1152]{1,0:T(8,128)(2,1)}) %all-gather.5.cloned.1.call-update) | async-done | bytes 5308432 | tf_op jit(solution)/shard_map/all_gather | solution.py:151
  468.0 3.4 reduce_sum.52
  (108 shorter events, 43.0 us)
Async XLA Ops:
  7.2 18.0 %copy-start.25 = (bf16[1,160,1152]{2,1,0:T(8,128)(2,1)S(1)}, bf16[1,160,1152]{2,1,0:T(8,128)(2,1)}, u32[]{:S(2)}) copy-start(bf16[1,160,1152]{2,1,0:T(8,128)(2,1)} %param.12) | copy-start | bytes 1105924
  7.2 120.3 %all-gather.7.cloned.1.call-start = ((), (), s32[]{:S(2)}) async-start(), calls=%async_computation.11 | async-start | bytes 3041280 | tf_op jit(solution)/shard_map/all_gather | solution.py:107
  9.9 33.2 %all-to-all-start.1 = ((bf16[1,16,10,1152]{3,2,0,1:T(8,128)(2,1)}), bf16[1,16,10,1152]{3,2,0,1:T(8,128)(2,1)S(1)}, u32[]{:S(2)}, u32[]{:S(2)}) async-start(bf16[1,16,10,1152]{3,2,0,1:T(8,128)(2,1)} %bitcast.5), calls=%async_computation.1 | async-start | bytes 1179648 | tf_op jit(solution)/shard_map/all_to_all | solution.py:122
  25.2 25.8 %copy-start.26 = (bf16[1,160,1152]{2,1,0:T(8,128)(2,1)S(1)}, bf16[1,160,1152]{2,1,0:T(8,128)(2,1)}, u32[]{:S(2)}) copy-start(bf16[1,160,1152]{2,1,0:T(8,128)(2,1)} %param.8) | copy-start | bytes 1105924
  25.2 26.0 %copy-start.27 = (bf16[1,160,1152]{2,1,0:T(8,128)(2,1)S(1)}, bf16[1,160,1152]{2,1,0:T(8,128)(2,1)}, u32[]{:S(2)}) copy-start(bf16[1,160,1152]{2,1,0:T(8,128)(2,1)} %param.9) | copy-start | bytes 1105924
  43.1 9.3 %copy-start.10 = (bf16[1,16,10,1152]{3,2,0,1:T(8,128)(2,1)}, bf16[1,16,10,1152]{3,2,0,1:T(8,128)(2,1)S(1)}, u32[]{:S(2)}) copy-start(bf16[1,16,10,1152]{3,2,0,1:T(8,128)(2,1)S(1)} %all-to-all-done.1) | copy-start | bytes 1105924
  43.1 9.3 %copy-start.28 = (bf16[1,160,1152]{2,1,0:T(8,128)(2,1)S(1)}, bf16[1,160,1152]{2,1,0:T(8,128)(2,1)}, u32[]{:S(2)}) copy-start(bf16[1,160,1152]{2,1,0:T(8,128)(2,1)} %param.10) | copy-start | bytes 1105924
  43.1 23.8 %all-to-all-start.2 = ((bf16[1,16,10,1152]{3,2,0,1:T(8,128)(2,1)}), bf16[1,16,10,1152]{3,2,0,1:T(8,128)(2,1)S(1)}, u32[]{:S(2)}, u32[]{:S(2)}) async-start(bf16[1,16,10,1152]{3,2,0,1:T(8,128)(2,1)} %bitcast.6), calls=%async_computation.2 | async-start | bytes 1179648 | tf_op jit(solution)/shard_map/all_to_all | solution.py:123
  51.2 24.7 %copy-start.7 = (bf16[1,160,1152]{1,2,0:T(8,128)(2,1)}, bf16[1,160,1152]{1,2,0:T(8,128)(2,1)S(1)}, u32[]{:S(2)}) copy-start(bf16[1,160,1152]{1,2,0:T(8,128)(2,1)S(1)} %copy.131) | copy-start | bytes 1105924
  66.9 9.0 %copy-start.13 = (bf16[1,16,10,1152]{3,2,0,1:T(8,128)(2,1)}, bf16[1,16,10,1152]{3,2,0,1:T(8,128)(2,1)S(1)}, u32[]{:S(2)}) copy-start(bf16[1,16,10,1152]{3,2,0,1:T(8,128)(2,1)S(1)} %all-to-all-done.2) | copy-start | bytes 1105924
  66.9 23.7 %all-to-all-start.3 = ((bf16[1,16,10,1152]{3,2,0,1:T(8,128)(2,1)}), bf16[1,16,10,1152]{3,2,0,1:T(8,128)(2,1)}, u32[]{:S(2)}, u32[]{:S(2)}) async-start(bf16[1,16,10,1152]{3,2,0,1:T(8,128)(2,1)} %bitcast.7), calls=%async_computation.3 | async-start | bytes 1179648 | tf_op jit(solution)/shard_map/all_to_all | solution.py:124
  82.4 17.8 %copy-start.30 = (bf16[1,160,1152]{2,1,0:T(8,128)(2,1)S(1)}, bf16[1,160,1152]{2,1,0:T(8,128)(2,1)}, u32[]{:S(2)}) copy-start(bf16[1,160,1152]{2,1,0:T(8,128)(2,1)} %param.15) | copy-start | bytes 1105924
  84.2 17.0 %copy-start.11 = (bf16[1,16,10,1152]{3,2,0,1:T(8,128)(2,1)S(1)}, bf16[1,16,10,1152]{3,2,0,1:T(8,128)(2,1)}, u32[]{:S(2)}) copy-start(bf16[1,16,10,1152]{3,2,0,1:T(8,128)(2,1)} %copy-done.10) | copy-start | bytes 1105924
  90.6 23.8 %all-to-all-start = ((bf16[1,16,10,1152]{3,2,0,1:T(8,128)(2,1)}), bf16[1,16,10,1152]{3,2,0,1:T(8,128)(2,1)S(1)}, u32[]{:S(2)}, u32[]{:S(2)}) async-start(bf16[1,16,10,1152]{3,2,0,1:T(8,128)(2,1)} %bitcast.3), calls=%async_computation | async-start | bytes 1179648 | tf_op jit(solution)/shard_map/all_to_all | solution.py:125
  102.4 6.0 %copy-start.3 = (bf16[16,10,16,72]{3,2,1,0:T(8,128)(2,1)}, bf16[16,10,16,72]{3,2,1,0:T(8,128)(2,1)S(1)}, u32[]{:S(2)}) copy-start(bf16[16,10,16,72]{3,2,1,0:T(8,128)(2,1)S(1)} %reshape.180) | copy-start | bytes 1105924
  103.6 4.7 copy-start.5
  106.2 17.6 %copy-start.18 = (bf16[16,10,16,72]{3,2,1,0:T(8,128)(2,1)}, bf16[16,10,16,72]{3,2,1,0:T(8,128)(2,1)S(1)}, u32[]{:S(2)}) copy-start(bf16[16,10,16,72]{3,2,1,0:T(8,128)(2,1)S(1)} %reshape.182) | copy-start | bytes 1105924
  114.4 22.7 %all-to-all-start.4 = ((bf16[1,16,10,1152]{3,2,0,1:T(8,128)(2,1)}), bf16[1,16,10,1152]{3,2,0,1:T(8,128)(2,1)S(1)}, u32[]{:S(2)}, u32[]{:S(2)}) async-start(bf16[1,16,10,1152]{3,2,0,1:T(8,128)(2,1)} %bitcast.10), calls=%async_computation.4 | async-start | bytes 1179648 | tf_op jit(solution)/shard_map/all_to_all | solution.py:126
  123.6 237.0 %reduce-scatter.4.cloned.1.call-start = ((), (), s32[]{:S(2)}) async-start(), calls=%async_computation.12 | async-start | bytes 2820096
  142.1 218.5 %copy-start.23 = (bf16[16,10,1152]{2,0,1:T(8,128)(2,1)S(1)}, bf16[16,10,1152]{2,0,1:T(8,128)(2,1)}, u32[]{:S(2)}) copy-start(bf16[16,10,1152]{2,0,1:T(8,128)(2,1)} %copy-done.22) | copy-start | bytes 1105924
  142.1 325.8 %all-gather.5.cloned.1.call-start = ((), (), s32[]{:S(2)}) async-start(), calls=%async_computation.10 | async-start | bytes 5474304 | tf_op jit(solution)/shard_map/all_gather | solution.py:151
  362.5 7.9 %copy-start.17 = (f32[10,16,16,16]{2,3,1,0:T(8,128)S(1)}, f32[10,16,16,16]{2,3,1,0:T(8,128)}, u32[]{:S(2)}) copy-start(f32[10,16,16,16]{2,3,1,0:T(8,128)} %get-tuple-element.29) | copy-start | bytes 491524
  362.5 20.1 %all-to-all-start.5 = ((bf16[16,10,1152]{2,1,0:T(8,128)(2,1)}), bf16[16,10,1152]{2,1,0:T(8,128)(2,1)S(1)}, u32[]{:S(2)}, u32[]{:S(2)}) async-start(bf16[16,10,1152]{2,1,0:T(8,128)(2,1)} %copy.94), calls=%async_computation.5 | async-start | bytes 1179648 | tf_op jit(solution)/shard_map/all_to_all | solution.py:132
  382.6 7.3 %copy-start.12 = (bf16[16,10,1152]{2,1,0:T(8,128)(2,1)}, bf16[16,10,1152]{2,1,0:T(8,128)(2,1)S(1)}, u32[]{:S(2)}) copy-start(bf16[16,10,1152]{2,1,0:T(8,128)(2,1)S(1)} %all-to-all-done.5) | copy-start | bytes 1105924
  382.6 19.4 %all-to-all-start.8 = ((bf16[16,10,1152]{2,1,0:T(8,128)(2,1)}), bf16[16,10,1152]{2,1,0:T(8,128)(2,1)}, u32[]{:S(2)}, u32[]{:S(2)}) async-start(bf16[16,10,1152]{2,1,0:T(8,128)(2,1)} %reshape.178), calls=%async_computation.8 | async-start | bytes 1179648 | tf_op jit(solution)/shard_map/all_to_all | solution.py:135
  394.8 15.5 %copy-start.1 = (f32[16,160,160]{1,2,0:T(8,128)S(1)}, f32[16,160,160]{1,2,0:T(8,128)}, u32[]{:S(2)}) copy-start(f32[16,160,160]{1,2,0:T(8,128)} %copy-done) | copy-start | bytes 4915204
  402.0 21.9 %all-to-all-start.7 = ((bf16[16,10,1152]{2,1,0:T(8,128)(2,1)}), bf16[16,10,1152]{2,1,0:T(8,128)(2,1)S(1)}, u32[]{:S(2)}, u32[]{:S(2)}) async-start(bf16[16,10,1152]{2,1,0:T(8,128)(2,1)} %reshape.177), calls=%async_computation.7 | async-start | bytes 1179648 | tf_op jit(solution)/shard_map/all_to_all | solution.py:134
  412.4 17.5 %copy-start.21 = (bf16[160,16,72]{0,2,1:T(8,128)(2,1)S(1)}, bf16[160,16,72]{0,2,1:T(8,128)(2,1)}, u32[]{:S(2)}) copy-start(bf16[160,16,72]{0,2,1:T(8,128)(2,1)} %copy.95) | copy-start | bytes 1105924
  423.9 9.2 %copy-start.15 = (bf16[16,10,1152]{2,1,0:T(8,128)(2,1)}, bf16[16,10,1152]{2,1,0:T(8,128)(2,1)S(1)}, u32[]{:S(2)}) copy-start(bf16[16,10,1152]{2,1,0:T(8,128)(2,1)S(1)} %all-to-all-done.7) | copy-start | bytes 1105924
  423.9 19.8 %all-to-all-start.6 = ((bf16[16,10,1152]{2,1,0:T(8,128)(2,1)}), bf16[16,10,1152]{2,1,0:T(8,128)(2,1)}, u32[]{:S(2)}, u32[]{:S(2)}) async-start(bf16[16,10,1152]{2,1,0:T(8,128)(2,1)} %reshape.176), calls=%async_computation.6 | async-start | bytes 1179648 | tf_op jit(solution)/shard_map/all_to_all | solution.py:133
  429.9 5.2 %copy-start.9 = (bf16[1,160,1152]{1,2,0:T(8,128)(2,1)S(1)}, bf16[1,160,1152]{1,2,0:T(8,128)(2,1)}, u32[]{:S(2)}) copy-start(bf16[1,160,1152]{1,2,0:T(8,128)(2,1)} %copy.132) | copy-start | bytes 1105924
  437.0 2.9 copy-start.16
  (11 other events, 20.1 us)
Sparse Core Ops, SparseCore 0:
  10.2 98.2 all-gather.6
  142.2 218.2 reduce-scatter.3
  362.9 104.9 all-gather.4
